TPU v7x, 32 devices: a whole 2x2x4 slice. The times are simulated.
32 devices in a mesh: rows: 8 (over y, x, core), cols: 4 (over z).
Axes of the slice: x: 2, y: 2, z: 4, core: 2. Of those that a mesh axis runs over, the one named last changes fastest.
Arguments:
- snapshots: float32 [8192, 8192], P('rows', 'cols'), may hold values from -500 to 500, as said below
Outputs:
- updated: float32 [8192, 8192], P('rows', 'cols')
- coeffs: float32 [512, 8192], P(None, 'cols')
Inputs may be any that keep to these rules, and one draw needn't show every extreme that they name: `snapshots`: Real-valued entries.
All inputs are finite; a program needn't handle non-finite values.
Results may differ from a plain program's by a relative error of at most 0.000055.
Values sent between devices are 32-bit elements; how exact they have to be, the bound alone decides.
No kernel may reach another device: no remote copies, remote signals or barrier semaphores. Data moves between devices by JAX's collectives and lax.ppermute only.
A program may use at most 128 MiB of HBM per device.

v0:
```python
import jax
import jax.numpy as jnp
from jax import lax
from jax.sharding import PartitionSpec as P

PB = 512


def broadcast(block, axis, source):
    block = jnp.where(lax.axis_index(axis) == source, block, jnp.zeros_like(block))
    return lax.psum(block, axis)


def shards(snapshots):
    highest = lax.Precision.HIGHEST
    rows_dev, cols_dev = snapshots.shape
    total_rows = rows_dev * lax.axis_size("rows")
    panel = snapshots[:, :PB]
    local_gram = (
        jnp.dot(panel.T, panel, precision=highest, preferred_element_type=jnp.float32) / total_rows
    )
    gram = lax.psum(local_gram, "rows")
    lower = jnp.linalg.cholesky(gram)
    factor = lower.T
    basis = lax.linalg.triangular_solve(lower, panel, left_side=False, lower=True, transpose_a=True)
    basis = broadcast(basis, "cols", 0)
    partial_proj = (
        jnp.dot(basis.T, snapshots, precision=highest, preferred_element_type=jnp.float32)
        / total_rows
    )
    proj = lax.psum(partial_proj, "rows")
    column = lax.axis_index("cols") * cols_dev + jnp.arange(cols_dev, dtype=jnp.int32)
    is_panel = (column < PB)[None, :]
    coeff_fill = jnp.concatenate([factor, jnp.zeros((PB, cols_dev - PB), jnp.float32)], axis=1)
    coeffs = jnp.where(is_panel, coeff_fill, proj)
    trailing = snapshots - jnp.dot(
        basis, proj, precision=highest, preferred_element_type=jnp.float32
    )
    basis_fill = jnp.concatenate([basis, jnp.zeros((rows_dev, cols_dev - PB), jnp.float32)], axis=1)
    updated = jnp.where(is_panel, basis_fill, trailing)
    return (updated, coeffs)


def solution(mesh):
    in_specs = (P("rows", "cols"),)
    out_specs = (P("rows", "cols"), P(None, "cols"))
    return jax.shard_map(shards, mesh=mesh, in_specs=in_specs, out_specs=out_specs, check_vma=False)
```

profile of v0, /device:TPU:0, one launch (start us, length us, event | category | flops | bytes accessed | tf_op | source)
XLA Modules:
  0.0 450.0 jit_solution(13193877418435620194)
XLA Ops:
  7.2 6.7 %fusion.8 = f32[512,512]{0,1:T(8,128)} fusion(f32[1024,2048]{1,0:T(8,128)} %param.1), kind=kOutput, calls=%fused_computation.14 | convolution fusion | flops 3221487616 | bytes 3145728 | tf_op jit(solution)/shard_map/dot_general | solution.py:20
  14.2 59.2 %all-reduce.7.cloned.1.call-done = f32[512,512]{0,1:T(8,128)} async-done(((f32[512,512]{0,1:T(8,128)}), f32[512,512]{0,1:T(8,128)}) %all-reduce.7.cloned.1.call-update) | async-done | bytes 1048592 | tf_op jit(solution)/shard_map/psum | solution.py:22
  76.5 11.7 %cholesky.104 = f32[128,128]{1,0:T(8,128)S(1)} custom-call(f32[128,128]{1,0:T(8,128)S(1)} %cholesky.266), custom_call_target="Cholesky" | custom-call | tf_op jit(solution)/shard_map/jit(cholesky)/cholesky | solution.py:23
  88.2 9.8 %custom-call.30 = f32[1,128,128]{1,2,0:T(8,128)S(1)} custom-call(f32[1,128,128]{2,1,0:T(8,128)S(1)} %get-tuple-element.33), custom_call_target="InvertDiagBlocksLowerTriangular" | custom-call | tf_op jit(solution)/shard_map/jit(cholesky)/cholesky | solution.py:23
  98.8 11.7 %cholesky.217 = f32[128,128]{1,0:T(8,128)S(1)} custom-call(f32[128,128]{1,0:T(8,128)S(1)} %cholesky.270), custom_call_target="Cholesky" | custom-call | tf_op jit(solution)/shard_map/jit(cholesky)/cholesky | solution.py:23
  110.6 10.0 %custom-call.31 = f32[1,128,128]{1,2,0:T(8,128)S(1)} custom-call(f32[1,128,128]{2,1,0:T(8,128)S(1)} %get-tuple-element.30), custom_call_target="InvertDiagBlocksLowerTriangular" | custom-call | tf_op jit(solution)/shard_map/jit(cholesky)/cholesky | solution.py:23
  121.2 11.7 %cholesky.238 = f32[128,128]{1,0:T(8,128)S(1)} custom-call(f32[128,128]{1,0:T(8,128)S(1)} %cholesky.275), custom_call_target="Cholesky" | custom-call | tf_op jit(solution)/shard_map/jit(cholesky)/cholesky | solution.py:23
  133.7 9.8 %custom-call.32 = f32[1,128,128]{1,2,0:T(8,128)S(1)} custom-call(f32[1,128,128]{2,1,0:T(8,128)S(1)} %get-tuple-element.27), custom_call_target="InvertDiagBlocksLowerTriangular" | custom-call | tf_op jit(solution)/shard_map/jit(cholesky)/cholesky | solution.py:23
  144.1 11.7 %cholesky.255 = f32[128,128]{1,0:T(8,128)S(1)} custom-call(f32[128,128]{1,0:T(8,128)S(1)} %convolution_subtract_fusion.4), custom_call_target="Cholesky" | custom-call | tf_op jit(solution)/shard_map/jit(cholesky)/cholesky | solution.py:23
  160.4 8.5 %while.1 = (s32[]{:T(128)}, f32[512,512]{1,0:T(8,128)S(1)}, s32[4,2]{0,1:T(2,128)S(1)}, f32[4,128,128]{2,1,0:T(8,128)S(1)}, s32[]{:T(128)}) while((s32[]{:T(128)}, f32[512,512]{1,0:T(8,128)S(1)}, s32[4,2]{0,1:T(2,128)S(1)}, f32[4,128,128]{2,1,0:T(8,128)S(1)}, s32[]{:T(128)}) %tuple.33), condition=%wide.while_cond, body=%wide.while_body.sunk | while | flops 2 | bytes 131189 | solution.py:25
  168.9 39.3 %custom-call.33 = f32[4,128,128]{1,2,0:T(8,128)S(1)} custom-call(f32[4,128,128]{2,1,0:T(8,128)S(1)} %get-tuple-element.9), custom_call_target="InvertDiagBlocksLowerTriangular" | custom-call | tf_op jit(solution)/shard_map/triangular_solve | solution.py:25
  208.2 1.7 fusion.20
  209.9 2.0 convolution_subtract_fusion.1
  212.6 2.9 convolution_subtract_fusion
  216.1 3.8 fusion.11
  220.5 1.6 maximum_select_fusion
  222.3 85.5 %all-reduce.9.cloned.1.call-done = f32[1024,512]{0,1:T(8,128)} async-done(((f32[1024,512]{0,1:T(8,128)}), f32[1024,512]{0,1:T(8,128)}) %all-reduce.9.cloned.1.call-update) | async-done | bytes 2097168 | tf_op jit(solution)/shard_map/psum | solution.py:11
  307.8 17.7 %convolution_multiply_fusion = f32[512,2048]{0,1:T(8,128)} fusion(f32[1024,512]{0,1:T(8,128)} %all-reduce.9.cloned.1.call-done, f32[1024,2048]{1,0:T(8,128)} %param.1), kind=kOutput, calls=%fused_computation.4 | convolution fusion | flops 12885950464 | bytes 14680064 | tf_op jit(solution)/shard_map/dot_general | solution.py:28
  325.5 9.2 %copy.6 = f32[1024,2048]{0,1:T(8,128)} copy(f32[1024,2048]{1,0:T(8,128)} %param.1) | data formatting | bytes 16777216 | tf_op args[0]
  334.7 70.9 %all-reduce.11.cloned.1.call-done = f32[512,2048]{0,1:T(8,128)} async-done(((f32[512,2048]{0,1:T(8,128)}), f32[512,2048]{0,1:T(8,128)}) %all-reduce.11.cloned.1.call-update) | async-done | bytes 4194320 | tf_op jit(solution)/shard_map/psum | solution.py:31
  405.7 3.8 pad_select_fusion
  409.5 5.5 %copy.9 = f32[512,2048]{1,0:T(8,128)} copy(f32[512,2048]{0,1:T(8,128)} %pad_select_fusion) | data formatting | bytes 8388608
  414.9 19.2 %subtract_select_fusion = f32[1024,2048]{0,1:T(8,128)} fusion(f32[1024,2048]{0,1:T(8,128)} %copy.6, f32[1024,512]{0,1:T(8,128)S(1)} %copy-done, pred[2048]{0:T(1024)(128)(4,1)S(1)} %add_compare_fusion, f32[512,2048]{0,1:T(8,128)} %all-reduce.11.cloned.1.call-done), kind=kOutput, calls=%fused_computation.2 | convolution fusion | flops 12889096192 | bytes 23070720 | tf_op jit(solution)/shard_map/dot_general | solution.py:36
  434.1 9.1 %copy.8 = f32[1024,2048]{1,0:T(8,128)} copy(f32[1024,2048]{0,1:T(8,128)} %subtract_select_fusion) | data formatting | bytes 16777216
  (47 shorter events, 18.6 us)
Async XLA Ops:
  7.2 66.3 %all-reduce.7.cloned.1.call-start = ((), (), s32[]{:S(2)}) async-start(), calls=%async_computation | async-start | bytes 2097152 | tf_op jit(solution)/shard_map/psum | solution.py:22
  14.0 293.9 %all-reduce.9.cloned.1.call-start = ((), (), s32[]{:S(2)}) async-start(), calls=%async_computation.1 | async-start | bytes 4194304 | tf_op jit(solution)/shard_map/psum | solution.py:11
  222.1 183.5 %all-reduce.11.cloned.1.call-start = ((), (), s32[]{:S(2)}) async-start(), calls=%async_computation.2 | async-start | bytes 8388608 | tf_op jit(solution)/shard_map/psum | solution.py:31
  409.5 5.5 %copy-start = (f32[1024,512]{0,1:T(8,128)S(1)}, f32[1024,512]{0,1:T(8,128)}, u32[]{:S(2)}) copy-start(f32[1024,512]{0,1:T(8,128)} %all-reduce.9.cloned.1.call-done) | copy-start | bytes 6291460
Sparse Core Ops, SparseCore 0:
  14.1 59.3 all-reduce.6
  222.2 85.5 all-reduce.8
  325.7 79.9 all-reduce.10
where the time goes:
time: 454 us; the launch traced here: 450 us
  waiting for transfers between devices  216 us (48%)
  other arithmetic  125 us (28%)
  matrix products  57.7 us (13%)
  local copies, waits for them, and re-layouts  33.9 us (7%)
  between operations  16.7 us (4%)
    psum x1, waiting for transfers between devices, broadcast(): return lax.psum(block, axis)  85.5 us
    another operation x14, other arithmetic, shards(): lower = jnp.linalg.cholesky(gram)  78.6 us
    psum x1, waiting for transfers between devices, shards(): proj = lax.psum(partial_proj, 'rows')  70.9 us
    psum x1, waiting for transfers between devices, shards(): gram = lax.psum(local_gram, 'rows')  59.2 us
    another operation x2, other arithmetic, shards(): lax.linalg.triangular_solve(lower, panel, left_side=False, lower=True, tr...  39.3 us
    unnamed x5, local copies, waits for them, and re-layouts  23.8 us
    dot_general x1, matrix products, shards(): jnp.dot(basis, proj, precision=highest, preferred_element_type=jnp.float32)  19.2 us
    dot_general x1, matrix products, shards(): jnp.dot(basis.T, snapshots, precision=highest, preferred_element_type=jnp...  17.7 us
  transfers between devices with their start and end apart: 3, of which 3 were waited for; matrix products, arithmetic and copies ran while one was open for 2% of the time, Pallas kernels for 0%

commit v1 on v0

--- a/solution.py
+++ b/solution.py
@@ -28,7 +28,9 @@
         jnp.dot(basis.T, snapshots, precision=highest, preferred_element_type=jnp.float32)
         / total_rows
     )
-    proj = lax.psum(partial_proj, "rows")
+    proj = partial_proj
+    for hop in (1, 2, 4):
+        proj = proj + lax.ppermute(proj, "rows", [(dev, dev ^ hop) for dev in range(8)])
     column = lax.axis_index("cols") * cols_dev + jnp.arange(cols_dev, dtype=jnp.int32)
     is_panel = (column < PB)[None, :]
     coeff_fill = jnp.concatenate([factor, jnp.zeros((PB, cols_dev - PB), jnp.float32)], axis=1)

time: 454 us -> 571 us (1.26)
  waiting for transfers between devices: 216 us -> 325 us
  other arithmetic: 125 us -> 131 us
    ppermute x0 -> x3, waiting for transfers between devices: none -> 180 us  [shards(): lax.ppermute(proj, 'rows', [(dev, dev ^ hop) for dev in range(8)])]
    psum x1 -> x0, waiting for transfers between devices: 70.9 us -> none  [shards(): proj = lax.psum(partial_proj, 'rows')]
  transfers between devices with their start and end apart: 3 -> 5, of which waited for: 3 -> 5; matrix products, arithmetic and copies ran while one was open for 2% -> 2% of each run, Pallas kernels for 0% -> 0%
where the time goes in v1:
time: 571 us; the launch traced here: 567 us
  waiting for transfers between devices  325 us (57%)
  other arithmetic  131 us (23%)
  matrix products  57.1 us (10%)
  local copies, waits for them, and re-layouts  33.9 us (6%)
  between operations  17 us (3%)
    ppermute x3, waiting for transfers between devices, shards(): lax.ppermute(proj, 'rows', [(dev, dev ^ hop) for dev in range(8)])  180 us
    psum x1, waiting for transfers between devices, broadcast(): return lax.psum(block, axis)  85.7 us
    another operation x14, other arithmetic, shards(): lower = jnp.linalg.cholesky(gram)  78.6 us
    psum x1, waiting for transfers between devices, shards(): gram = lax.psum(local_gram, 'rows')  59.2 us
    another operation x2, other arithmetic, shards(): lax.linalg.triangular_solve(lower, panel, left_side=False, lower=True, tr...  39.3 us
    unnamed x5, local copies, waits for them, and re-layouts  23.9 us
    dot_general x1, matrix products, shards(): jnp.dot(basis, proj, precision=highest, preferred_element_type=jnp.float32)  19.6 us
    dot_general x1, matrix products, shards(): jnp.dot(basis.T, snapshots, precision=highest, preferred_element_type=jnp...  16.6 us
  transfers between devices with their start and end apart: 5, of which 5 were waited for; matrix products, arithmetic and copies ran while one was open for 2% of the time, Pallas kernels for 0%

profile of v1, /device:TPU:0, one launch (start us, length us, event | category | flops | bytes accessed | tf_op | source)
XLA Modules:
  0.0 566.9 jit_solution(11015083892864941306)
XLA Ops:
  7.2 6.7 %fusion.9 = f32[512,512]{0,1:T(8,128)} fusion(f32[1024,2048]{1,0:T(8,128)} %param.1), kind=kOutput, calls=%fused_computation.15 | convolution fusion | flops 3221487616 | bytes 3145728 | tf_op jit(solution)/shard_map/dot_general | solution.py:20
  14.2 59.2 %all-reduce.6.cloned.1.call-done = f32[512,512]{0,1:T(8,128)} async-done(((f32[512,512]{0,1:T(8,128)}), f32[512,512]{0,1:T(8,128)}) %all-reduce.6.cloned.1.call-update) | async-done | bytes 1048592 | tf_op jit(solution)/shard_map/psum | solution.py:22
  76.5 11.7 %cholesky.104 = f32[128,128]{1,0:T(8,128)S(1)} custom-call(f32[128,128]{1,0:T(8,128)S(1)} %cholesky.266), custom_call_target="Cholesky" | custom-call | tf_op jit(solution)/shard_map/jit(cholesky)/cholesky | solution.py:23
  88.2 9.8 %custom-call.30 = f32[1,128,128]{1,2,0:T(8,128)S(1)} custom-call(f32[1,128,128]{2,1,0:T(8,128)S(1)} %get-tuple-element.33), custom_call_target="InvertDiagBlocksLowerTriangular" | custom-call | tf_op jit(solution)/shard_map/jit(cholesky)/cholesky | solution.py:23
  98.8 11.7 %cholesky.217 = f32[128,128]{1,0:T(8,128)S(1)} custom-call(f32[128,128]{1,0:T(8,128)S(1)} %cholesky.270), custom_call_target="Cholesky" | custom-call | tf_op jit(solution)/shard_map/jit(cholesky)/cholesky | solution.py:23
  110.6 10.0 %custom-call.31 = f32[1,128,128]{1,2,0:T(8,128)S(1)} custom-call(f32[1,128,128]{2,1,0:T(8,128)S(1)} %get-tuple-element.30), custom_call_target="InvertDiagBlocksLowerTriangular" | custom-call | tf_op jit(solution)/shard_map/jit(cholesky)/cholesky | solution.py:23
  121.2 11.7 %cholesky.238 = f32[128,128]{1,0:T(8,128)S(1)} custom-call(f32[128,128]{1,0:T(8,128)S(1)} %cholesky.275), custom_call_target="Cholesky" | custom-call | tf_op jit(solution)/shard_map/jit(cholesky)/cholesky | solution.py:23
  133.7 9.8 %custom-call.32 = f32[1,128,128]{1,2,0:T(8,128)S(1)} custom-call(f32[1,128,128]{2,1,0:T(8,128)S(1)} %get-tuple-element.27), custom_call_target="InvertDiagBlocksLowerTriangular" | custom-call | tf_op jit(solution)/shard_map/jit(cholesky)/cholesky | solution.py:23
  144.1 11.7 %cholesky.255 = f32[128,128]{1,0:T(8,128)S(1)} custom-call(f32[128,128]{1,0:T(8,128)S(1)} %convolution_subtract_fusion.4), custom_call_target="Cholesky" | custom-call | tf_op jit(solution)/shard_map/jit(cholesky)/cholesky | solution.py:23
  160.4 8.5 %while.1 = (s32[]{:T(128)}, f32[512,512]{1,0:T(8,128)S(1)}, s32[4,2]{0,1:T(2,128)S(1)}, f32[4,128,128]{2,1,0:T(8,128)S(1)}, s32[]{:T(128)}) while((s32[]{:T(128)}, f32[512,512]{1,0:T(8,128)S(1)}, s32[4,2]{0,1:T(2,128)S(1)}, f32[4,128,128]{2,1,0:T(8,128)S(1)}, s32[]{:T(128)}) %tuple.33), condition=%wide.while_cond, body=%wide.while_body.sunk | while | flops 2 | bytes 131189 | solution.py:25
  168.9 39.3 %custom-call.33 = f32[4,128,128]{1,2,0:T(8,128)S(1)} custom-call(f32[4,128,128]{2,1,0:T(8,128)S(1)} %get-tuple-element.9), custom_call_target="InvertDiagBlocksLowerTriangular" | custom-call | tf_op jit(solution)/shard_map/triangular_solve | solution.py:25
  212.6 2.9 convolution_subtract_fusion
  216.1 3.8 fusion.12
  222.1 85.7 %all-reduce.8.cloned.1.call-done = f32[1024,512]{0,1:T(8,128)} async-done(((f32[1024,512]{0,1:T(8,128)}), f32[1024,512]{0,1:T(8,128)}) %all-reduce.8.cloned.1.call-update) | async-done | bytes 2097168 | tf_op jit(solution)/shard_map/psum | solution.py:11
  307.8 16.6 %convolution_multiply_fusion = f32[512,2048]{0,1:T(8,128)S(1)} fusion(f32[1024,512]{0,1:T(8,128)} %all-reduce.8.cloned.1.call-done, f32[1024,2048]{1,0:T(8,128)} %param.1), kind=kOutput, calls=%fused_computation.4 | convolution fusion | flops 12885950464 | bytes 14680064 | tf_op jit(solution)/shard_map/dot_general | solution.py:28
  324.5 7.1 %collective-permute-done = f32[512,2048]{0,1:T(8,128)S(1)} collective-permute-done((f32[512,2048]{0,1:T(8,128)S(1)}, f32[512,2048]{0,1:T(8,128)S(1)}, u32[]{:S(2)}, u32[]{:S(2)}) %collective-permute-start) | collective-permute-done | bytes 4194336 | tf_op jit(solution)/shard_map/ppermute | solution.py:33
  334.2 91.1 %collective-permute-done.1 = f32[512,2048]{0,1:T(8,128)S(1)} collective-permute-done((f32[512,2048]{0,1:T(8,128)S(1)}, f32[512,2048]{0,1:T(8,128)S(1)}, u32[]{:S(2)}, u32[]{:S(2)}) %collective-permute-start.1) | collective-permute-done | bytes 4194336 | tf_op jit(solution)/shard_map/ppermute | solution.py:33
  425.3 3.0 add.71
  429.8 9.2 %copy.6 = f32[1024,2048]{0,1:T(8,128)} copy(f32[1024,2048]{1,0:T(8,128)} %param.1) | data formatting | bytes 16777216 | tf_op args[0]
  439.0 81.4 %collective-permute-done.2 = f32[512,2048]{0,1:T(8,128)} collective-permute-done((f32[512,2048]{0,1:T(8,128)}, f32[512,2048]{0,1:T(8,128)}, u32[]{:S(2)}, u32[]{:S(2)}) %collective-permute-start.2) | collective-permute-done | bytes 4194336 | tf_op jit(solution)/shard_map/ppermute | solution.py:33
  520.4 5.1 pad_select_fusion
  525.5 5.5 copy.9
  531.0 19.6 %subtract_select_fusion = f32[1024,2048]{0,1:T(8,128)} fusion(f32[1024,2048]{0,1:T(8,128)} %copy.6, f32[1024,512]{0,1:T(8,128)S(1)} %copy-done, pred[2048]{0:T(1024)(128)(4,1)S(1)} %add_compare_fusion, f32[512,2048]{0,1:T(8,128)} %add.71, f32[512,2048]{0,1:T(8,128)} %collective-permute-done.2), kind=kOutput, calls=%fused_computation.2 | convolution fusion | flops 12890144768 | bytes 27265024 | tf_op jit(solution)/shard_map/dot_general | solution.py:38
  550.7 9.1 %copy.8 = f32[1024,2048]{1,0:T(8,128)} copy(f32[1024,2048]{0,1:T(8,128)} %subtract_select_fusion) | data formatting | bytes 16777216
  (52 shorter events, 27.8 us)
Async XLA Ops:
  7.2 66.3 %all-reduce.6.cloned.1.call-start = ((), (), s32[]{:S(2)}) async-start(), calls=%async_computation | async-start | bytes 2097152 | tf_op jit(solution)/shard_map/psum | solution.py:22
  14.0 293.9 %all-reduce.8.cloned.1.call-start = ((), (), s32[]{:S(2)}) async-start(), calls=%async_computation.1 | async-start | bytes 4194304 | tf_op jit(solution)/shard_map/psum | solution.py:11
  324.4 7.2 %collective-permute-start = (f32[512,2048]{0,1:T(8,128)S(1)}, f32[512,2048]{0,1:T(8,128)S(1)}, u32[]{:S(2)}, u32[]{:S(2)}) collective-permute-start(f32[512,2048]{0,1:T(8,128)S(1)} %convolution_multiply_fusion), channel_id=1, source_target_pairs={{0,4},{4,0},{8,12},{12,8},{16,20},{20,16},{24,28},{28,24},{1,5},{5... | collective-permute-start | bytes 12582920 | tf_op jit(solution)/shard_map/ppermute | solution.py:33
  332.6 92.7 %collective-permute-start.1 = (f32[512,2048]{0,1:T(8,128)S(1)}, f32[512,2048]{0,1:T(8,128)S(1)}, u32[]{:S(2)}, u32[]{:S(2)}) collective-permute-start(f32[512,2048]{0,1:T(8,128)S(1)} %add.70), channel_id=1, source_target_pairs={{0,8},{4,12},{8,0},{12,4},{16,24},{20,28},{24,16},{28,20},{1,9},{5... | collective-permute-start | bytes 12582920 | tf_op jit(solution)/shard_map/ppermute | solution.py:33
  428.3 92.1 %collective-permute-start.2 = (f32[512,2048]{0,1:T(8,128)}, f32[512,2048]{0,1:T(8,128)}, u32[]{:S(2)}, u32[]{:S(2)}) collective-permute-start(f32[512,2048]{0,1:T(8,128)} %add.71), channel_id=1, source_target_pairs={{0,16},{4,20},{8,24},{12,28},{16,0},{20,4},{24,8},{28,12},{1,17},{... | collective-permute-start | bytes 12582920 | tf_op jit(solution)/shard_map/ppermute | solution.py:33
  525.5 5.5 copy-start
Sparse Core Ops, SparseCore 0:
  14.1 59.3 all-reduce.5
  222.2 85.5 all-reduce.7
